TPU v7x, 32 devices: a whole 2x2x4 slice. The times are simulated.
32 devices in a mesh: dp: 8 (over y, x, core), tensor: 4 (over z).
Axes of the slice: x: 2, y: 2, z: 4, core: 2. Of those that a mesh axis runs over, the one named last changes fastest.
Arguments:
- tokens: bfloat16 [8, 736, 1152], P('dp', 'tensor'), may hold values from -45 to 45
- key_mask: int32 [8, 736], P('dp'), may hold values from 0 to 1, as said below
- query_weight: bfloat16 [1152, 1152], P('dp', 'tensor'), may hold values from -0.1875 to 0.1875
- key_weight: bfloat16 [1152, 1152], P('dp', 'tensor'), may hold values from -0.1875 to 0.1875
- value_weight: bfloat16 [1152, 1152], P('dp', 'tensor'), may hold values from -0.1875 to 0.1875
- out_weight: bfloat16 [1152, 1152], P('tensor', 'dp'), may hold values from -0.375 to 0.375
- up_weight: bfloat16 [1152, 4304], P('dp', 'tensor'), may hold values from -0.1875 to 0.1875
- down_weight: bfloat16 [4304, 1152], P('tensor', 'dp'), may hold values from -0.09375 to 0.09375
- first_gain: bfloat16 [1152], P('dp'), may hold values from 0.5 to 1.5
- first_shift: bfloat16 [1152], P('dp'), may hold values from -3 to 3
- query_bias: bfloat16 [1152], P('dp'), may hold values from -3 to 3
- value_bias: bfloat16 [1152], P('dp'), may hold values from -3 to 3
- out_bias: bfloat16 [1152], P('dp'), may hold values from -3 to 3
- second_gain: bfloat16 [1152], P('dp'), may hold values from 0.5 to 1.5
- second_shift: bfloat16 [1152], P('dp'), may hold values from -3 to 3
- up_bias: bfloat16 [4304], P('dp'), may hold values from -3 to 3
- down_bias: bfloat16 [1152], P('dp'), may hold values from -3 to 3
- cotangent: bfloat16 [8, 736, 1152], P('dp', 'tensor'), may hold values from -6 to 6
Outputs:
- output: bfloat16 [8, 736, 1152], P('dp', 'tensor')
- input_grad: float32 [8, 736, 1152], P('dp', 'tensor')
- query_grad: float32 [1152, 1152], P('dp', 'tensor')
- key_grad: float32 [1152, 1152], P('dp', 'tensor')
- value_grad: float32 [1152, 1152], P('dp', 'tensor')
- out_grad: float32 [1152, 1152], P('tensor', 'dp')
- up_grad: float32 [1152, 4304], P('dp', 'tensor')
- down_grad: float32 [4304, 1152], P('tensor', 'dp')
- first_gain_grad: float32 [1152], P('dp')
- first_shift_grad: float32 [1152], P('dp')
- query_bias_grad: float32 [1152], P('dp')
- value_bias_grad: float32 [1152], P('dp')
- out_bias_grad: float32 [1152], P('dp')
- second_gain_grad: float32 [1152], P('dp')
- second_shift_grad: float32 [1152], P('dp')
- up_bias_grad: float32 [4304], P('dp')
- down_bias_grad: float32 [1152], P('dp')
Inputs may be any that keep to these rules, and one draw needn't show every extreme that they name: `key_mask`: each image's ones form a prefix of its positions, at least its first three quarters.
All inputs are finite; a program needn't handle non-finite values.
Results may differ from a plain program's by a relative error of at most 0.017.
The roundings to bfloat16 on the way count: a program that leaves them out, or rounds other values in their place, can miss the bound.
Values may be sent and summed in bfloat16 or wider, within the bound.
A program may use at most 128 MiB of HBM per device.

v0:
```python
from functools import partial
import math
import jax
import jax.numpy as jnp
from jax import lax
from jax.sharding import PartitionSpec as P

HD = 72
EPSILON = 1e-06
GELU_COEF = 0.7978845608028654
MASK_FILL = -1e30


def norm_forward(inputs, gain_vec, shift_vec):
    centred = inputs - jnp.mean(inputs, axis=-1, keepdims=True)
    inv_std = lax.rsqrt(jnp.mean(centred * centred, axis=-1, keepdims=True) + EPSILON)
    normed = centred * inv_std
    return (normed * gain_vec + shift_vec, normed, inv_std)


def norm_backward(grad_in, normed, inv_std, gain_vec):
    scaled = grad_in * gain_vec
    return inv_std * (
        scaled
        - jnp.mean(scaled, axis=-1, keepdims=True)
        - normed * jnp.mean(scaled * normed, axis=-1, keepdims=True)
    )


def gelu_pair(pre_act):
    tanh_val = jnp.tanh(GELU_COEF * (pre_act + 0.044715 * pre_act * pre_act * pre_act))
    gelu_value = 0.5 * pre_act * (1.0 + tanh_val)
    gelu_slope = 0.5 * (1.0 + tanh_val) + 0.5 * pre_act * (
        1.0 - tanh_val * tanh_val
    ) * GELU_COEF * (1.0 + 3.0 * 0.044715 * pre_act * pre_act)
    return (gelu_value, gelu_slope)


def mat_dot(left, right):
    return jnp.dot(left, right, preferred_element_type=jnp.float32)


def gather_rows(local):
    return lax.all_gather(local, "tensor", axis=1, tiled=True)


def sum_rows(partial_term):
    return lax.psum_scatter(
        partial_term.astype(jnp.bfloat16), "tensor", scatter_dimension=1, tiled=True
    ).astype(jnp.float32)


def attend_image(packed):
    query_img, keys_img, values_img, valid_img = packed
    scores = jnp.einsum("qhd,khd->hqk", query_img, keys_img, preferred_element_type=jnp.float32)
    scores = jnp.where(valid_img[None, None, :] > 0, scores, MASK_FILL)
    highest = jnp.max(scores, axis=-1, keepdims=True)
    logsum = highest + jnp.log(jnp.sum(jnp.exp(scores - highest), axis=-1, keepdims=True))
    probs = jnp.exp(scores - logsum).astype(jnp.bfloat16)
    mixed = jnp.einsum("hqk,khd->qhd", probs, values_img, preferred_element_type=jnp.float32)
    return (mixed.astype(jnp.bfloat16), logsum[..., 0])


def attend_back(scale_factor, packed):
    query_img, keys_img, values_img, valid_img, logsum_img, mixed_img, grad_img = packed
    scores = jnp.einsum("qhd,khd->hqk", query_img, keys_img, preferred_element_type=jnp.float32)
    scores = jnp.where(valid_img[None, None, :] > 0, scores, MASK_FILL)
    probs_full = jnp.exp(scores - logsum_img[:, :, None])
    probs = probs_full.astype(jnp.bfloat16)
    grad_values = jnp.einsum("hqk,qhd->khd", probs, grad_img, preferred_element_type=jnp.float32)
    grad_probs = jnp.einsum(
        "qhd,khd->hqk", grad_img, values_img, preferred_element_type=jnp.float32
    )
    delta = jnp.sum(grad_img.astype(jnp.float32) * mixed_img.astype(jnp.float32), axis=-1).T
    grad_scores = (probs_full * (grad_probs - delta[:, :, None])).astype(jnp.bfloat16)
    grad_query = (
        jnp.einsum("hqk,khd->qhd", grad_scores, keys_img, preferred_element_type=jnp.float32)
        * scale_factor
    )
    grad_keys = jnp.einsum(
        "hqk,qhd->khd", grad_scores, query_img, preferred_element_type=jnp.float32
    )
    return (grad_query, grad_keys, grad_values)


def vector_share(full_vec, parts, index):
    piece = full_vec.shape[0] // parts
    return lax.dynamic_slice_in_dim(full_vec, index * piece, piece)


def shards(
    tokens,
    key_mask,
    query_weight,
    key_weight,
    value_weight,
    out_weight,
    up_weight,
    down_weight,
    first_gain,
    first_shift,
    query_bias,
    value_bias,
    out_bias,
    second_gain,
    second_shift,
    up_bias,
    down_bias,
    cotangent,
):
    dp_count = lax.axis_size("dp")
    dp_index = lax.axis_index("dp")
    tensor_index = lax.axis_index("tensor")
    images = tokens.shape[0]
    width = tokens.shape[2]
    fetched = (
        lax.all_gather(query_weight, "dp", axis=0, tiled=True),
        lax.all_gather(key_weight, "dp", axis=0, tiled=True),
        lax.all_gather(value_weight, "dp", axis=0, tiled=True),
        lax.all_gather(out_weight, "dp", axis=1, tiled=True),
        lax.all_gather(up_weight, "dp", axis=0, tiled=True),
        lax.all_gather(down_weight, "dp", axis=1, tiled=True),
        lax.all_gather(first_gain, "dp", axis=0, tiled=True),
        lax.all_gather(first_shift, "dp", axis=0, tiled=True),
        lax.all_gather(query_bias, "dp", axis=0, tiled=True),
        lax.all_gather(value_bias, "dp", axis=0, tiled=True),
        lax.all_gather(out_bias, "dp", axis=0, tiled=True),
        lax.all_gather(second_gain, "dp", axis=0, tiled=True),
        lax.all_gather(second_shift, "dp", axis=0, tiled=True),
        lax.all_gather(up_bias, "dp", axis=0, tiled=True),
        lax.all_gather(down_bias, "dp", axis=0, tiled=True),
    )
    query_full, key_full, value_full, out_full, up_full, down_full = fetched[:6]
    (
        gain_one,
        shift_one,
        query_bias_all,
        value_bias_all,
        out_bias_all,
        gain_two,
        shift_two,
        up_bias_all,
        down_bias_all,
    ) = [member.astype(jnp.float32) for member in fetched[6:]]
    head_cols = query_full.shape[1]
    hidden_cols = up_full.shape[1]
    heads_local = head_cols // HD
    query_bias_local = lax.dynamic_slice_in_dim(query_bias_all, tensor_index * head_cols, head_cols)
    value_bias_local = lax.dynamic_slice_in_dim(value_bias_all, tensor_index * head_cols, head_cols)
    up_bias_local = lax.dynamic_slice_in_dim(up_bias_all, tensor_index * hidden_cols, hidden_cols)
    scale_factor = 1.0 / math.sqrt(HD)
    inputs = tokens.astype(jnp.float32)
    first, normed_one, inv_one = norm_forward(inputs, gain_one, shift_one)
    first_rows = gather_rows(first.astype(jnp.bfloat16))
    seq_full = first_rows.shape[1]
    row_shape = (images, seq_full, width)
    head_shape = (images, seq_full, heads_local, HD)
    first_flat = first_rows.reshape(-1, width)
    query = (
        ((mat_dot(first_flat, query_full) + query_bias_local) * scale_factor)
        .astype(jnp.bfloat16)
        .reshape(head_shape)
    )
    keys = mat_dot(first_flat, key_full).astype(jnp.bfloat16).reshape(head_shape)
    values = (
        (mat_dot(first_flat, value_full) + value_bias_local)
        .astype(jnp.bfloat16)
        .reshape(head_shape)
    )
    mixed, logsum = lax.map(attend_image, (query, keys, values, key_mask))
    mixed_flat = mixed.reshape(-1, head_cols)
    hidden = inputs + sum_rows(mat_dot(mixed_flat, out_full).reshape(row_shape)) + out_bias_all
    second, normed_two, inv_two = norm_forward(hidden, gain_two, shift_two)
    second_flat = gather_rows(second.astype(jnp.bfloat16)).reshape(-1, width)
    pre_act = mat_dot(second_flat, up_full) + up_bias_local
    gelu_value, gelu_slope = gelu_pair(pre_act)
    act = gelu_value.astype(jnp.bfloat16)
    output = (hidden + sum_rows(mat_dot(act, down_full).reshape(row_shape)) + down_bias_all).astype(
        jnp.bfloat16
    )
    query_back, key_back, value_back, out_back, up_back, down_back = (
        lax.all_gather(query_weight, "dp", axis=0, tiled=True),
        lax.all_gather(key_weight, "dp", axis=0, tiled=True),
        lax.all_gather(value_weight, "dp", axis=0, tiled=True),
        lax.all_gather(out_weight, "dp", axis=1, tiled=True),
        lax.all_gather(up_weight, "dp", axis=0, tiled=True),
        lax.all_gather(down_weight, "dp", axis=1, tiled=True),
    )
    grad_out = cotangent.astype(jnp.float32)
    down_bias_grad = jnp.sum(grad_out, axis=(0, 1))
    grad_rows = gather_rows(cotangent).reshape(-1, width)
    down_grad = mat_dot(act.T, grad_rows)
    grad_pre = mat_dot(grad_rows, down_back.T) * gelu_slope
    up_bias_part = jnp.sum(grad_pre, axis=0)
    grad_pre_low = grad_pre.astype(jnp.bfloat16)
    up_grad = mat_dot(second_flat.T, grad_pre_low)
    grad_second = sum_rows(mat_dot(grad_pre_low, up_back.T).reshape(row_shape))
    second_gain_grad = jnp.sum(grad_second * normed_two, axis=(0, 1))
    second_shift_grad = jnp.sum(grad_second, axis=(0, 1))
    grad_hidden = grad_out + norm_backward(grad_second, normed_two, inv_two, gain_two)
    out_bias_grad = jnp.sum(grad_hidden, axis=(0, 1))
    hidden_rows = gather_rows(grad_hidden.astype(jnp.bfloat16)).reshape(-1, width)
    grad_mixed = mat_dot(hidden_rows, out_back.T).astype(jnp.bfloat16)
    out_grad = mat_dot(mixed_flat.T, hidden_rows)
    grad_query_f, grad_keys_f, grad_values_f = lax.map(
        partial(attend_back, scale_factor),
        (query, keys, values, key_mask, logsum, mixed, grad_mixed.reshape(head_shape)),
    )
    grad_query_f = grad_query_f.reshape(-1, head_cols)
    grad_keys_f = grad_keys_f.reshape(-1, head_cols)
    grad_values_f = grad_values_f.reshape(-1, head_cols)
    query_bias_part = jnp.sum(grad_query_f, axis=0)
    value_bias_part = jnp.sum(grad_values_f, axis=0)
    grad_query = grad_query_f.astype(jnp.bfloat16)
    grad_keys = grad_keys_f.astype(jnp.bfloat16)
    grad_values = grad_values_f.astype(jnp.bfloat16)
    query_grad = mat_dot(first_flat.T, grad_query)
    key_grad = mat_dot(first_flat.T, grad_keys)
    value_grad = mat_dot(first_flat.T, grad_values)
    first_term = (
        mat_dot(grad_query, query_back.T)
        + mat_dot(grad_keys, key_back.T)
        + mat_dot(grad_values, value_back.T)
    )
    grad_first = sum_rows(first_term.reshape(row_shape))
    first_gain_grad = jnp.sum(grad_first * normed_one, axis=(0, 1))
    first_shift_grad = jnp.sum(grad_first, axis=(0, 1))
    input_grad = grad_hidden + norm_backward(grad_first, normed_one, inv_one, gain_one)
    matrix_shares = (
        lax.psum_scatter(query_grad, "dp", scatter_dimension=0, tiled=True),
        lax.psum_scatter(key_grad, "dp", scatter_dimension=0, tiled=True),
        lax.psum_scatter(value_grad, "dp", scatter_dimension=0, tiled=True),
        lax.psum_scatter(out_grad, "dp", scatter_dimension=1, tiled=True),
        lax.psum_scatter(up_grad, "dp", scatter_dimension=0, tiled=True),
        lax.psum_scatter(down_grad, "dp", scatter_dimension=1, tiled=True),
    )
    query_bias_full = lax.dynamic_update_slice_in_dim(
        jnp.zeros((width,), jnp.float32), query_bias_part, tensor_index * head_cols, 0
    )
    value_bias_full = lax.dynamic_update_slice_in_dim(
        jnp.zeros((width,), jnp.float32), value_bias_part, tensor_index * head_cols, 0
    )
    up_bias_full = lax.dynamic_update_slice_in_dim(
        jnp.zeros((up_bias_all.shape[0],), jnp.float32), up_bias_part, tensor_index * hidden_cols, 0
    )
    vector_sums = lax.psum(
        (
            first_gain_grad,
            first_shift_grad,
            query_bias_full,
            value_bias_full,
            out_bias_grad,
            second_gain_grad,
            second_shift_grad,
            up_bias_full,
            down_bias_grad,
        ),
        ("dp", "tensor"),
    )
    vector_parts = tuple((vector_share(member, dp_count, dp_index) for member in vector_sums))
    return (output, input_grad) + tuple(matrix_shares) + vector_parts


def solution(mesh):
    return jax.shard_map(
        shards,
        mesh=mesh,
        in_specs=(
            P("dp", "tensor", None),
            P("dp", None),
            P("dp", "tensor"),
            P("dp", "tensor"),
            P("dp", "tensor"),
            P("tensor", "dp"),
            P("dp", "tensor"),
            P("tensor", "dp"),
            P("dp"),
            P("dp"),
            P("dp"),
            P("dp"),
            P("dp"),
            P("dp"),
            P("dp"),
            P("dp"),
            P("dp"),
            P("dp", "tensor", None),
        ),
        out_specs=(
            P("dp", "tensor", None),
            P("dp", "tensor", None),
            P("dp", "tensor"),
            P("dp", "tensor"),
            P("dp", "tensor"),
            P("tensor", "dp"),
            P("dp", "tensor"),
            P("tensor", "dp"),
            P("dp"),
            P("dp"),
            P("dp"),
            P("dp"),
            P("dp"),
            P("dp"),
            P("dp"),
            P("dp"),
            P("dp"),
        ),
        check_vma=False,
    )
```

profile of v0, /device:TPU:0, one launch (start us, length us, event | category | flops | bytes accessed | tf_op | source)
XLA Modules:
  0.0 748.6 jit_solution(14068338893583376241)
XLA Ops:
  8.1 1.3 dynamic-slice.1
  10.7 1.1 convert_reduce_fusion.2
  11.9 1.3 fusion.70
  13.2 0.9 dynamic-update-slice.3
  14.0 0.8 dynamic-update-slice.2
  14.9 0.8 dynamic-update-slice
  15.7 0.8 dynamic-update-slice.1
  19.1 0.8 dynamic-update-slice.8
  19.9 0.9 dynamic-update-slice.7
  20.8 26.1 %all-reduce.14 = (bf16[1152]{0:T(1024)(128)(2,1)S(1)}, bf16[1152]{0:T(1024)(128)(2,1)S(1)}, bf16[1152]{0:T(1024)(128)(2,1)S(1)}, bf16[1152]{0:T(1024)(128)(2,1)S...) all-reduce(bf16[1152]{0:T(1024)(128)(2,1)S(1)} %dynamic-update-slic, ...), channel_id=1, replica_groups=mesh['dp'=8,'tensor'=4] {'dp'}, use_global_device_ids=true, to_apply=%add.6 | all-reduce | flops 13520 | bytes 54080
  46.9 2.0 fusion.66
  49.9 10.0 %all_gather.68 = bf16[1152,288]{1,0:T(8,128)(2,1)S(1)} all-gather(bf16[144,288]{1,0:T(8,128)(2,1)} %param.20), channel_id=1, replica_groups=mesh['dp'=8,'tensor'=4] {'dp'}, dimensions={0}, use_global_device_ids=true | all-gather | bytes 746496 | tf_op jit(solution)/shard_map/all_gather | solution.py:117
  59.9 10.5 %all_gather.70 = bf16[1152,288]{1,0:T(8,128)(2,1)S(1)} all-gather(bf16[144,288]{1,0:T(8,128)(2,1)S(1)} %copy-done.18), channel_id=1, replica_groups=mesh['dp'=8,'tensor'=4] {'dp'}, dimensions={0}, use_global_device_ids=true | all-gather | bytes 746496 | tf_op jit(solution)/shard_map/all_gather | solution.py:118
  70.4 10.2 %all_gather.66 = bf16[1152,288]{1,0:T(8,128)(2,1)S(1)} all-gather(bf16[144,288]{1,0:T(8,128)(2,1)S(1)} %copy-done.19), channel_id=1, replica_groups=mesh['dp'=8,'tensor'=4] {'dp'}, dimensions={0}, use_global_device_ids=true | all-gather | bytes 746496 | tf_op jit(solution)/shard_map/all_gather | solution.py:119
  80.5 11.5 %all_gather.71 = bf16[288,1152]{0,1:T(8,128)(2,1)} all-gather(bf16[288,144]{0,1:T(8,128)(2,1)S(1)} %copy-done.20), channel_id=1, replica_groups=mesh['dp'=8,'tensor'=4] {'dp'}, dimensions={1}, use_global_device_ids=true | all-gather | bytes 746496 | tf_op jit(solution)/shard_map/all_gather | solution.py:120
  92.0 2.4 fusion.49
  95.3 1.7 select_reduce_fusion
  97.0 1.8 exponential_reduce_fusion
  100.4 1.9 convolution_convert_fusion.4
  103.1 2.4 fusion.10
  106.2 37.0 %reduce-scatter.35.cloned.1.call-done = bf16[1,184,1152]{2,1,0:T(8,128)(2,1)} async-done(((bf16[1,736,1152]{2,1,0:T(8,128)(2,1)}), bf16[1,184,1152]{2,1,0:T(8,128)(2,1)}) %reduce-scatter.35.cloned.1.call-update) | async-done | bytes 423952
  143.2 1.2 fusion.80
  144.5 1.3 multiply_reduce_fusion.1
  145.8 2.0 add_convert_fusion.1
  149.5 36.8 %all-gather.9.cloned.1.call-done = bf16[1,736,1152]{2,1,0:T(8,128)(2,1)} async-done(((bf16[1,184,1152]{2,1,0:T(8,128)(2,1)}), bf16[1,736,1152]{2,1,0:T(8,128)(2,1)}) %all-gather.9.cloned.1.call-update) | async-done | bytes 1695760 | tf_op jit(solution)/shard_map/all_gather | solution.py:44
  186.3 6.4 convolution_add_fusion.2
  192.8 32.8 %all-gather.15.cloned.1.call-done = bf16[1,736,1152]{2,1,0:T(8,128)(2,1)} async-done(((bf16[1,184,1152]{2,1,0:T(8,128)(2,1)}), bf16[1,736,1152]{2,1,0:T(8,128)(2,1)}) %all-gather.15.cloned.1.call-update) | async-done | bytes 1695760 | tf_op jit(solution)/shard_map/all_gather | solution.py:44
  225.6 30.9 %all-gather.13.cloned.1.call-done = bf16[1076,1152]{0,1:T(8,128)(2,1)} async-done(((bf16[1076,144]{0,1:T(8,128)(2,1)}), bf16[1076,1152]{0,1:T(8,128)(2,1)}) %all-gather.13.cloned.1.call-update) | async-done | bytes 2479120 | tf_op jit(solution)/shard_map/all_gather | solution.py:122
  256.5 8.2 %fusion.86 = (f32[1076]{0:T(1024)}, bf16[736,1076]{0,1:T(8,128)(2,1)S(1)}) fusion(f32[736,1076]{0,1:T(8,128)} %convolution_add_fusion.2, bf16[1076,1152]{0,1:T(8,128)(2,1)} %all-gather.13.cloned.1.call-done, bf16[1,736,1152]{2,1,0:T(8,128)(2,1)} %all-gather.15.cloned.1.call-done), kind=kOutput, calls=%fused_computation.117 | convolution fusion | flops 1840458240 | bytes 8930768 | tf_op jit(solution)/shard_map/dot_general | solution.py:40
  264.7 1.2 copy-done.29
  265.9 4.0 fusion.8
  269.9 7.2 fusion.7
  277.2 30.1 %reduce-scatter.39.cloned.1.call-done = bf16[1,184,1152]{2,1,0:T(8,128)(2,1)} async-done(((bf16[1,736,1152]{2,1,0:T(8,128)(2,1)}), bf16[1,184,1152]{2,1,0:T(8,128)(2,1)}) %reduce-scatter.39.cloned.1.call-update) | async-done | bytes 423952
  307.3 1.6 fusion.76
  309.5 36.8 %reduce-scatter.37.cloned.1.call-done = bf16[1,184,1152]{2,1,0:T(8,128)(2,1)} async-done(((bf16[1,736,1152]{2,1,0:T(8,128)(2,1)}), bf16[1,184,1152]{2,1,0:T(8,128)(2,1)}) %reduce-scatter.37.cloned.1.call-update) | async-done | bytes 423952
  346.3 2.7 fusion.83
  350.3 38.2 %all-gather.17.cloned.1.call-done = bf16[1,736,1152]{2,1,0:T(8,128)(2,1)} async-done(((bf16[1,184,1152]{2,1,0:T(8,128)(2,1)}), bf16[1,736,1152]{2,1,0:T(8,128)(2,1)}) %all-gather.17.cloned.1.call-update) | async-done | bytes 1695760 | tf_op jit(solution)/shard_map/all_gather | solution.py:44
  388.5 2.5 fusion.52
  391.0 1.2 multiply_reduce_fusion
  392.1 5.6 fusion.84
  397.8 5.6 multiply_convert_fusion
  403.4 1.4 convolution_convert_fusion.3
  404.9 1.0 fusion.85
  405.9 1.1 fusion.87
  407.2 1.2 convolution_add_fusion.1
  408.4 2.4 fusion.9
  410.8 7.4 fusion.15
  418.5 1.2 copy-done.26
  419.7 6.5 fusion.18
  426.2 0.9 copy-done.17
  427.2 3.9 fusion.11
  431.2 3.9 fusion.21
  435.2 3.9 fusion.25
  439.2 3.8 fusion.23
  444.0 2.7 reduce-scatter.41.cloned.1.call-done
  446.7 1.5 fusion.77
  448.2 41.8 %all-reduce.13 = (f32[1152]{0:T(1024)S(1)}, f32[1152]{0:T(1024)S(1)}, f32[1152]{0:T(1024)S(1)}, f32[1152]{0:T(1024)S(1)}, f32[1152]{0:T(1024)S(1)}, /*index=5*/f...) all-reduce(f32[1152]{0:T(1024)S(1)} %get-tuple-element.73, ...), channel_id=1, replica_groups=mesh['dp'=8,'tensor'=4] {'dp','tensor'}, use_global_device_ids=true, to_apply=%region_22.23 | all-reduce | flops 13520 | bytes 108160 | tf_op jit(solution)/shard_map/psum | solution.py:246
  495.8 2.2 fusion.69
  498.0 9.4 %reduce-scatter.33.cloned.1.call-done = f32[1076,144]{0,1:T(8,128)} async-done(((f32[1076,1152]{0,1:T(8,128)}), f32[1076,144]{0,1:T(8,128)}) %reduce-scatter.33.cloned.1.call-update) | async-done | bytes 619792 | tf_op jit(solution)/shard_map/reduce_scatter | solution.py:235
  507.5 61.1 %reduce-scatter.31.cloned.1.call-done = f32[144,1076]{1,0:T(8,128)} async-done(((f32[1152,1076]{1,0:T(8,128)}), f32[144,1076]{1,0:T(8,128)}) %reduce-scatter.31.cloned.1.call-update) | async-done | bytes 619792 | tf_op jit(solution)/shard_map/reduce_scatter | solution.py:234
  568.5 43.1 %reduce-scatter.29.cloned.1.call-done = f32[288,144]{0,1:T(8,128)} async-done(((f32[288,1152]{0,1:T(8,128)}), f32[288,144]{0,1:T(8,128)}) %reduce-scatter.29.cloned.1.call-update) | async-done | bytes 165904 | tf_op jit(solution)/shard_map/reduce_scatter | solution.py:233
  611.6 43.1 %reduce-scatter.27.cloned.1.call-done = f32[144,288]{1,0:T(8,128)} async-done(((f32[1152,288]{1,0:T(8,128)}), f32[144,288]{1,0:T(8,128)}) %reduce-scatter.27.cloned.1.call-update) | async-done | bytes 165904 | tf_op jit(solution)/shard_map/reduce_scatter | solution.py:232
  654.7 43.3 %reduce-scatter.23.cloned.1.call-done = f32[144,288]{1,0:T(8,128)} async-done(((f32[1152,288]{1,0:T(8,128)}), f32[144,288]{1,0:T(8,128)}) %reduce-scatter.23.cloned.1.call-update) | async-done | bytes 165904 | tf_op jit(solution)/shard_map/reduce_scatter | solution.py:230
  698.0 43.1 %reduce-scatter.25.cloned.1.call-done = f32[144,288]{1,0:T(8,128)} async-done(((f32[1152,288]{1,0:T(8,128)}), f32[144,288]{1,0:T(8,128)}) %reduce-scatter.25.cloned.1.call-update) | async-done | bytes 165904 | tf_op jit(solution)/shard_map/reduce_scatter | solution.py:231
  (141 shorter events, 18.6 us)
Async XLA Ops:
  8.0 51.8 %copy-start.18 = (bf16[144,288]{1,0:T(8,128)(2,1)S(1)}, bf16[144,288]{1,0:T(8,128)(2,1)}, u32[]{:S(2)}) copy-start(bf16[144,288]{1,0:T(8,128)(2,1)} %param.21) | copy-start | bytes 248836
  8.0 62.3 %copy-start.19 = (bf16[144,288]{1,0:T(8,128)(2,1)S(1)}, bf16[144,288]{1,0:T(8,128)(2,1)}, u32[]{:S(2)}) copy-start(bf16[144,288]{1,0:T(8,128)(2,1)} %param.22) | copy-start | bytes 248836
  8.0 72.5 %copy-start.20 = (bf16[288,144]{0,1:T(8,128)(2,1)S(1)}, bf16[288,144]{0,1:T(8,128)(2,1)}, u32[]{:S(2)}) copy-start(bf16[288,144]{0,1:T(8,128)(2,1)} %param.23) | copy-start | bytes 248836
  8.1 84.0 %all-gather.7.cloned.1.call-start = ((), (), s32[]{:S(2)}) async-start(), calls=%async_computation.10 | async-start | bytes 2119680 | tf_op jit(solution)/shard_map/all_gather | solution.py:44
  48.9 94.3 %reduce-scatter.35.cloned.1.call-start = ((), (), s32[]{:S(2)}) async-start(), calls=%async_computation.22 | async-start | bytes 2119680
  70.4 24.9 %copy-start.3 = (bf16[1152,288]{1,0:T(8,128)(2,1)}, bf16[1152,288]{1,0:T(8,128)(2,1)S(1)}, u32[]{:S(2)}) copy-start(bf16[1152,288]{1,0:T(8,128)(2,1)S(1)} %all_gather.70) | copy-start | bytes 1990660
  92.0 2.4 copy-start.25
  94.4 2.6 copy-start.7
  95.3 1.8 copy-start.9
  97.0 3.4 copy-start.1
  98.8 3.5 copy-start.21
  99.6 2.7 copy-start.27
  100.4 2.6 copy-start.13
  102.3 0.8 copy-start.16
  102.3 40.9 %copy-start = (bf16[1,184,1152]{2,1,0:T(8,128)(2,1)S(1)}, bf16[1,184,1152]{2,1,0:T(8,128)(2,1)}, u32[]{:S(2)}) copy-start(bf16[1,184,1152]{2,1,0:T(8,128)(2,1)} %param.18) | copy-start | bytes 1271812
  105.5 44.0 %all-gather.11.cloned.1.call-start = ((), (), s32[]{:S(2)}) async-start(), calls=%async_computation.12 | async-start | bytes 2985984 | tf_op jit(solution)/shard_map/all_gather | solution.py:121
  106.1 80.2 %all-gather.9.cloned.1.call-start = ((), (), s32[]{:S(2)}) async-start(), calls=%async_computation.11 | async-start | bytes 2119680 | tf_op jit(solution)/shard_map/all_gather | solution.py:44
  147.8 77.8 %all-gather.15.cloned.1.call-start = ((), (), s32[]{:S(2)}) async-start(), calls=%async_computation.14 | async-start | bytes 2119680 | tf_op jit(solution)/shard_map/all_gather | solution.py:44
  148.4 108.1 %all-gather.13.cloned.1.call-start = ((), (), s32[]{:S(2)}) async-start(), calls=%async_computation.13 | async-start | bytes 2985984 | tf_op jit(solution)/shard_map/all_gather | solution.py:122
  149.1 158.2 %reduce-scatter.39.cloned.1.call-start = ((), (), s32[]{:S(2)}) async-start(), calls=%async_computation.24 | async-start | bytes 2119680
  256.5 9.4 %copy-start.24 = (bf16[1152,1076]{1,0:T(8,128)(2,1)S(1)}, bf16[1152,1076]{1,0:T(8,128)(2,1)}, u32[]{:S(2)}) copy-start(bf16[1152,1076]{1,0:T(8,128)(2,1)} %all-gather.11.cloned.1.call-done) | copy-start | bytes 7437316
  264.7 1.2 copy-start.29
  269.9 37.4 %copy-start.2 = (bf16[1,184,1152]{2,1,0:T(8,128)(2,1)S(1)}, bf16[1,184,1152]{2,1,0:T(8,128)(2,1)}, u32[]{:S(2)}) copy-start(bf16[1,184,1152]{2,1,0:T(8,128)(2,1)} %reduce-scatter.35.cloned.1.call-done) | copy-start | bytes 1271812
  269.9 76.4 %reduce-scatter.37.cloned.1.call-start = ((), (), s32[]{:S(2)}) async-start(), calls=%async_computation.23 | async-start | bytes 2119680
  277.2 111.3 %all-gather.17.cloned.1.call-start = ((), (), s32[]{:S(2)}) async-start(), calls=%async_computation.15 | async-start | bytes 2119680 | tf_op jit(solution)/shard_map/all_gather | solution.py:44
  348.9 43.2 %copy-start.22 = (f32[4,736]{1,0:T(4,128)S(1)}, f32[4,736]{1,0:T(4,128)}, u32[]{:S(2)}) copy-start(f32[4,736]{1,0:T(4,128)} %copy-done.21) | copy-start | bytes 35332
  349.8 96.9 %reduce-scatter.41.cloned.1.call-start = ((), (), s32[]{:S(2)}) async-start(), calls=%async_computation.25 | async-start | bytes 2119680
  392.1 5.7 copy-start.28
  397.8 10.6 %copy-start.14 = (bf16[736,4,72]{0,2,1:T(8,128)(2,1)}, bf16[736,4,72]{0,2,1:T(8,128)(2,1)S(1)}, u32[]{:S(2)}) copy-start(bf16[736,4,72]{0,2,1:T(8,128)(2,1)S(1)} %get-tuple-element.100) | copy-start | bytes 1271812
  397.8 5.6 copy-start.10
  403.4 1.5 copy-start.8
  404.9 2.2 copy-start.11
  405.9 1.2 copy-start.5
  405.9 1.3 copy-start.4
  410.8 96.7 %reduce-scatter.33.cloned.1.call-start = ((), (), s32[]{:S(2)}) async-start(), calls=%async_computation.21 | async-start | bytes 5971968 | tf_op jit(solution)/shard_map/reduce_scatter | solution.py:235
  418.2 1.5 copy-start.26
  418.2 150.3 %reduce-scatter.31.cloned.1.call-start = ((), (), s32[]{:S(2)}) async-start(), calls=%async_computation.20 | async-start | bytes 5971968 | tf_op jit(solution)/shard_map/reduce_scatter | solution.py:234
  426.1 1.0 copy-start.17
  426.2 5.0 copy-start.15
  426.2 185.4 %reduce-scatter.29.cloned.1.call-start = ((), (), s32[]{:S(2)}) async-start(), calls=%async_computation.19 | async-start | bytes 1990656 | tf_op jit(solution)/shard_map/reduce_scatter | solution.py:233
  431.1 4.1 copy-start.6
  431.1 223.6 %reduce-scatter.27.cloned.1.call-start = ((), (), s32[]{:S(2)}) async-start(), calls=%async_computation.18 | async-start | bytes 1990656 | tf_op jit(solution)/shard_map/reduce_scatter | solution.py:232
  435.1 4.1 copy-start.12
  435.1 262.8 %reduce-scatter.23.cloned.1.call-start = ((), (), s32[]{:S(2)}) async-start(), calls=%async_computation.16 | async-start | bytes 1990656 | tf_op jit(solution)/shard_map/reduce_scatter | solution.py:230
  439.1 3.9 copy-start.23
  439.1 302.0 %reduce-scatter.25.cloned.1.call-start = ((), (), s32[]{:S(2)}) async-start(), calls=%async_computation.17 | async-start | bytes 1990656 | tf_op jit(solution)/shard_map/reduce_scatter | solution.py:231
Sparse Core Ops, SparseCore 0:
  49.1 38.4 all-gather.6
  105.7 37.5 reduce-scatter.34
  270.0 37.2 reduce-scatter.38
  309.5 36.7 reduce-scatter.36
  349.9 38.5 all-gather.16
Sparse Core Ops, SparseCore 1:
  107.9 30.3 all-gather.10
  147.9 38.4 all-gather.8
  187.8 37.8 all-gather.14
  227.5 28.9 all-gather.12
  410.9 35.8 reduce-scatter.40
  450.7 56.7 reduce-scatter.32
  511.7 56.8 reduce-scatter.30
  572.3 39.2 reduce-scatter.28
  615.4 39.2 reduce-scatter.26
  658.7 39.2 reduce-scatter.22
  701.8 39.2 reduce-scatter.24
where the time goes:
time: 754 us; the launch traced here: 749 us
  waiting for transfers between devices  490 us (65%)
  blocking collectives  110 us (15%)
  matrix products  86 us (11%)
  other arithmetic  22.3 us (3%)
  local copies, waits for them, and re-layouts  20.8 us (3%)
  between operations  17.6 us (2%)
    unnamed x20, waiting for transfers between devices  109 us
    all_gather x4, waiting for transfers between devices, gather_rows(): return lax.all_gather(local, 'tensor', axis=1, tiled=True)  108 us
    dot_general x18, matrix products, mat_dot(): return jnp.dot(left, right, preferred_element_type=jnp.float32)  68.7 us
    reduce_scatter x1, waiting for transfers between devices, shards(): lax.psum_scatter(up_grad, 'dp', scatter_dimension=0, tiled=True)  61.1 us
    reduce_scatter x1, waiting for transfers between devices, shards(): lax.psum_scatter(query_grad, 'dp', scatter_dimension=0, tiled=True)  43.3 us
    reduce_scatter x1, waiting for transfers between devices, shards(): lax.psum_scatter(key_grad, 'dp', scatter_dimension=0, tiled=True)  43.1 us
    reduce_scatter x1, waiting for transfers between devices, shards(): lax.psum_scatter(value_grad, 'dp', scatter_dimension=0, tiled=True)  43.1 us
    reduce_scatter x1, waiting for transfers between devices, shards(): lax.psum_scatter(out_grad, 'dp', scatter_dimension=1, tiled=True)  43.1 us
  transfers between devices with their start and end apart: 16, of which 14 were waited for; matrix products, arithmetic and copies ran while one was open for 8% of the time, Pallas kernels for 0%

commit v1 on v0

--- a/solution.py
+++ b/solution.py
@@ -9,6 +9,18 @@
 EPSILON = 1e-06
 GELU_COEF = 0.7978845608028654
 MASK_FILL = -1e30
+
+
+def doubled_up(value, axis, dim):
+    ways, here, lap = (lax.axis_size(axis), lax.axis_index(axis), value.shape[dim])
+    line, have = (value, 1)
+    while have < ways:
+        line = jnp.concatenate(
+            [line, lax.ppermute(line, axis, [(d, (d - have) % ways) for d in range(ways)])],
+            axis=dim,
+        )
+        have = 2 * have
+    return jnp.roll(line, here * lap, axis=dim)
 
 
 def norm_forward(inputs, gain_vec, shift_vec):
@@ -41,7 +53,7 @@
 
 
 def gather_rows(local):
-    return lax.all_gather(local, "tensor", axis=1, tiled=True)
+    return doubled_up(local, "tensor", 1)
 
 
 def sum_rows(partial_term):

time: 754 us -> 795 us (1.054)
  other arithmetic: 22.3 us -> 48.3 us
  starting transfers between devices: 1.54 us -> 15.7 us
    ppermute x0 -> x8, waiting for transfers between devices: none -> 126 us  [doubled_up(): lax.ppermute(line, axis, [(d, (d - have) % ways) for d in range(ways)])]
    all_gather x4 -> x0, waiting for transfers between devices: 108 us -> none  [gather_rows(): return lax.all_gather(local, 'tensor', axis=1, tiled=True)]
    reduce_scatter x1, waiting for transfers between devices: 9.44 us -> 60.9 us  [shards(): lax.psum_scatter(down_grad, 'dp', scatter_dimension=1, tiled=True)]
    reduce_scatter x1, waiting for transfers between devices: 43.1 us -> 0.01 us  [shards(): lax.psum_scatter(out_grad, 'dp', scatter_dimension=1, tiled=True)]
    all_gather x1, waiting for transfers between devices: 30.9 us -> 0.01 us  [shards(): lax.all_gather(down_weight, 'dp', axis=1, tiled=True)]
    reshape x0 -> x4, other arithmetic: none -> 27.8 us  [the longest x1 7.42 us: shards(): grad_rows = gather_rows(cotangent).reshape(-1, width)]
    ppermute x0 -> x8, starting transfers between devices: none -> 14.8 us  [doubled_up(): lax.ppermute(line, axis, [(d, (d - have) % ways) for d in range(ways)])]
    dot_general x1, matrix products: 1.86 us -> 12.8 us  [attend_image(): jnp.einsum('hqk,khd->qhd', probs, values_img, preferred_element_type=jnp....]
  transfers between devices with their start and end apart: 16 -> 20, of which waited for: 14 -> 15; matrix products, arithmetic and copies ran while one was open for 8% -> 10% of each run, Pallas kernels for 0% -> 0%
where the time goes in v1:
time: 795 us; the launch traced here: 789 us
  waiting for transfers between devices  484 us (61%)
  blocking collectives  111 us (14%)
  matrix products  91.4 us (11%)
  other arithmetic  48.3 us (6%)
  local copies, waits for them, and re-layouts  21.5 us (3%)
  between operations  17.8 us (2%)
  starting transfers between devices  15.7 us (2%)
    ppermute x8, waiting for transfers between devices, doubled_up(): lax.ppermute(line, axis, [(d, (d - have) % ways) for d in range(ways)])  126 us
    unnamed x16, waiting for transfers between devices  114 us
    dot_general x18, matrix products, mat_dot(): return jnp.dot(left, right, preferred_element_type=jnp.float32)  65.3 us
    reduce_scatter x1, waiting for transfers between devices, shards(): lax.psum_scatter(up_grad, 'dp', scatter_dimension=0, tiled=True)  61.2 us
    reduce_scatter x1, waiting for transfers between devices, shards(): lax.psum_scatter(down_grad, 'dp', scatter_dimension=1, tiled=True)  60.9 us
    reduce_scatter x1, waiting for transfers between devices, shards(): lax.psum_scatter(query_grad, 'dp', scatter_dimension=0, tiled=True)  43.4 us
    reduce_scatter x1, waiting for transfers between devices, shards(): lax.psum_scatter(key_grad, 'dp', scatter_dimension=0, tiled=True)  43.4 us
    psum x1, blocking collectives, shards(): lax.psum((first_gain_grad, first_shift_grad, query_bias_full, value_bias_...  41.7 us
  transfers between devices with their start and end apart: 20, of which 15 were waited for; matrix products, arithmetic and copies ran while one was open for 10% of the time, Pallas kernels for 0%

profile of v1, /device:TPU:0, one launch (start us, length us, event | category | flops | bytes accessed | tf_op | source)
XLA Modules:
  0.0 789.0 jit_solution(2423756653553187605)
XLA Ops:
  8.1 1.4 dynamic-slice.1
  10.8 1.1 convert_reduce_fusion.2
  11.9 1.3 fusion.54
  20.9 26.1 %all-reduce.14 = (bf16[1152]{0:T(1024)(128)(2,1)S(1)}, bf16[1152]{0:T(1024)(128)(2,1)S(1)}, bf16[1152]{0:T(1024)(128)(2,1)S(1)}, bf16[1152]{0:T(1024)(128)(2,1)S...) all-reduce(bf16[1152]{0:T(1024)(128)(2,1)S(1)} %dynamic-update-slic, ...), channel_id=1, replica_groups=mesh['dp'=8,'tensor'=4] {'dp'}, use_global_device_ids=true, to_apply=%add.6 | all-reduce | flops 13520 | bytes 54080
  46.9 1.3 fusion.50
  48.2 3.7 collective-permute-start
  51.9 8.4 %collective-permute-done = bf16[1,184,1152]{2,1,0:T(8,128)(2,1)S(1)} collective-permute-done((bf16[1,184,1152]{2,1,0:T(8,128)(2,1)S(1)}, bf16[1,184,1152]{2,1,0:T(8,128)(2,1)S(1)}, u32[]{:S(2)}, u32[]{:S(2)}) %collective-permute-start) | collective-permute-done | bytes 423968 | tf_op jit(solution)/shard_map/ppermute | solution.py:19
  60.6 11.1 %all_gather.55 = bf16[1152,288]{1,0:T(8,128)(2,1)S(1)} all-gather(bf16[144,288]{1,0:T(8,128)(2,1)S(1)} %copy-done.22), channel_id=1, replica_groups=mesh['dp'=8,'tensor'=4] {'dp'}, dimensions={0}, use_global_device_ids=true | all-gather | bytes 746496 | tf_op jit(solution)/shard_map/all_gather | solution.py:129
  71.7 10.7 %all_gather.57 = bf16[1152,288]{1,0:T(8,128)(2,1)S(1)} all-gather(bf16[144,288]{1,0:T(8,128)(2,1)S(1)} %copy-done.23), channel_id=1, replica_groups=mesh['dp'=8,'tensor'=4] {'dp'}, dimensions={0}, use_global_device_ids=true | all-gather | bytes 746496 | tf_op jit(solution)/shard_map/all_gather | solution.py:130
  82.4 10.0 %all_gather.53 = bf16[1152,288]{1,0:T(8,128)(2,1)S(1)} all-gather(bf16[144,288]{1,0:T(8,128)(2,1)S(1)} %copy-done.24), channel_id=1, replica_groups=mesh['dp'=8,'tensor'=4] {'dp'}, dimensions={0}, use_global_device_ids=true | all-gather | bytes 746496 | tf_op jit(solution)/shard_map/all_gather | solution.py:131
  92.4 11.0 %all_gather.58 = bf16[288,1152]{0,1:T(8,128)(2,1)S(1)} all-gather(bf16[288,144]{0,1:T(8,128)(2,1)S(1)} %copy-done.25), channel_id=1, replica_groups=mesh['dp'=8,'tensor'=4] {'dp'}, dimensions={1}, use_global_device_ids=true | all-gather | bytes 746496 | tf_op jit(solution)/shard_map/all_gather | solution.py:132
  103.5 6.5 fusion.32
  111.6 1.7 select_reduce_fusion
  113.4 1.8 exponential_reduce_fusion
  117.0 12.8 %convolution_convert_fusion.4 = bf16[4,72,736]{2,1,0:T(8,128)(2,1)S(1)} fusion(bf16[736,4,72]{0,2,1:T(8,128)(2,1)S(1)} %bitcast.107, f32[4,736,736]{1,2,0:T(8,128)S(1)} %get-tuple-element.107, f32[4,736]{1,0:T(4,128)S(1)} %log_add_fusion, pred[736]{0:T(1024)(128)(4,1)S(1)} %compare_reduce_fusion), kind=kOutput, calls=%fused_computation.89 | convolution fusion | flops 318729216 | bytes 9527520 | tf_op jit(solution)/shard_map/while/body/eval_jaxpr/hqk,khd->qhd/dot_general | solution.py:72
  130.6 2.4 fusion.10
  134.2 3.0 collective-permute-start.4
  137.2 39.1 %reduce-scatter.35.cloned.1.call-done = bf16[1,184,1152]{2,1,0:T(8,128)(2,1)} async-done(((bf16[1,736,1152]{2,1,0:T(8,128)(2,1)}), bf16[1,184,1152]{2,1,0:T(8,128)(2,1)}) %reduce-scatter.35.cloned.1.call-update) | async-done | bytes 423952
  176.3 1.2 fusion.65
  177.5 1.3 multiply_reduce_fusion.1
  178.8 1.3 add_convert_fusion.1
  180.1 3.4 collective-permute-start.2
  184.5 9.2 %collective-permute-done.2 = bf16[1,184,1152]{2,1,0:T(8,128)(2,1)S(1)} collective-permute-done((bf16[1,184,1152]{2,1,0:T(8,128)(2,1)S(1)}, bf16[1,184,1152]{2,1,0:T(8,128)(2,1)S(1)}, u32[]{:S(2)}, u32[]{:S(2)}) %collective-permute-start.2) | collective-permute-done | bytes 423968 | tf_op jit(solution)/shard_map/ppermute | solution.py:19
  196.4 52.1 %collective-permute-done.5 = bf16[1,368,1152]{2,1,0:T(8,128)(2,1)} collective-permute-done((bf16[1,368,1152]{2,1,0:T(8,128)(2,1)}, bf16[1,368,1152]{2,1,0:T(8,128)(2,1)}, u32[]{:S(2)}, u32[]{:S(2)}) %collective-permute-start.5) | collective-permute-done | bytes 847904 | tf_op jit(solution)/shard_map/ppermute | solution.py:19
  248.6 7.4 fusion.20
  256.0 9.9 %collective-permute-done.3 = bf16[1,368,1152]{2,1,0:T(8,128)(2,1)} collective-permute-done((bf16[1,368,1152]{2,1,0:T(8,128)(2,1)}, bf16[1,368,1152]{2,1,0:T(8,128)(2,1)}, u32[]{:S(2)}, u32[]{:S(2)}) %collective-permute-start.3) | collective-permute-done | bytes 847904 | tf_op jit(solution)/shard_map/ppermute | solution.py:19
  265.9 7.4 fusion.26
  273.3 6.8 convolution_add_fusion.2
  280.1 8.2 %fusion.72 = (f32[1076]{0:T(1024)}, bf16[736,1076]{0,1:T(8,128)(2,1)S(1)}) fusion(f32[736,1076]{0,1:T(8,128)} %convolution_add_fusion.2, bf16[736,1152]{1,0:T(8,128)(2,1)} %fusion.20, bf16[1076,1152]{0,1:T(8,128)(2,1)} %all-gather.5.cloned.1.call-done), kind=kOutput, calls=%fused_computation.149 | convolution fusion | flops 1840458240 | bytes 8930768 | tf_op jit(solution)/shard_map/dot_general | solution.py:52
  288.3 1.2 copy-done.31
  289.5 3.9 fusion.8
  293.6 7.2 fusion.7
  301.0 30.5 %reduce-scatter.39.cloned.1.call-done = bf16[1,184,1152]{2,1,0:T(8,128)(2,1)} async-done(((bf16[1,736,1152]{2,1,0:T(8,128)(2,1)}), bf16[1,184,1152]{2,1,0:T(8,128)(2,1)}) %reduce-scatter.39.cloned.1.call-update) | async-done | bytes 423952
  331.5 1.6 fusion.60
  333.7 36.9 %reduce-scatter.37.cloned.1.call-done = bf16[1,184,1152]{2,1,0:T(8,128)(2,1)} async-done(((bf16[1,736,1152]{2,1,0:T(8,128)(2,1)}), bf16[1,184,1152]{2,1,0:T(8,128)(2,1)}) %reduce-scatter.37.cloned.1.call-update) | async-done | bytes 423952
  370.6 2.7 fusion.69
  373.3 1.6 collective-permute-start.6
  374.9 9.8 %collective-permute-done.6 = bf16[1,184,1152]{2,1,0:T(8,128)(2,1)S(1)} collective-permute-done((bf16[1,184,1152]{2,1,0:T(8,128)(2,1)S(1)}, bf16[1,184,1152]{2,1,0:T(8,128)(2,1)S(1)}, u32[]{:S(2)}, u32[]{:S(2)}) %collective-permute-start.6) | collective-permute-done | bytes 423968 | tf_op jit(solution)/shard_map/ppermute | solution.py:19
  384.8 2.2 collective-permute-start.7
  387.0 36.5 %collective-permute-done.7 = bf16[1,368,1152]{2,1,0:T(8,128)(2,1)S(1)} collective-permute-done((bf16[1,368,1152]{2,1,0:T(8,128)(2,1)S(1)}, bf16[1,368,1152]{2,1,0:T(8,128)(2,1)S(1)}, u32[]{:S(2)}, u32[]{:S(2)}) %collective-permute-start.7) | collective-permute-done | bytes 847904 | tf_op jit(solution)/shard_map/ppermute | solution.py:19
  423.5 6.5 fusion.14
  431.1 5.7 fusion.70
  436.8 3.5 multiply_convert_fusion
  440.3 1.4 convolution_convert_fusion.3
  441.8 1.0 fusion.71
  443.1 1.1 fusion.73
  444.3 1.2 convolution_add_fusion.1
  445.5 2.4 fusion.9
  448.0 3.8 fusion.77
  451.9 3.8 fusion.76
  455.7 3.8 fusion.74
  459.7 4.0 fusion.75
  463.7 7.0 fusion.66
  471.1 1.1 copy-done.13
  472.2 6.3 fusion.62
  480.1 6.1 reduce-scatter.41.cloned.1.call-done
  486.2 1.5 fusion.61
  487.7 41.7 %all-reduce.13 = (f32[1152]{0:T(1024)S(1)}, f32[1152]{0:T(1024)S(1)}, f32[1152]{0:T(1024)S(1)}, f32[1152]{0:T(1024)S(1)}, f32[1152]{0:T(1024)S(1)}, /*index=5*/f...) all-reduce(f32[1152]{0:T(1024)S(1)} %get-tuple-element.74, ...), channel_id=1, replica_groups=mesh['dp'=8,'tensor'=4] {'dp','tensor'}, use_global_device_ids=true, to_apply=%region_22.24 | all-reduce | flops 13520 | bytes 108160 | tf_op jit(solution)/shard_map/psum | solution.py:258
  535.1 2.2 fusion.53
  537.4 34.9 %reduce-scatter.27.cloned.1.call-done = f32[144,288]{1,0:T(8,128)} async-done(((f32[1152,288]{1,0:T(8,128)}), f32[144,288]{1,0:T(8,128)}) %reduce-scatter.27.cloned.1.call-update) | async-done | bytes 165904 | tf_op jit(solution)/shard_map/reduce_scatter | solution.py:244
  572.3 43.4 %reduce-scatter.23.cloned.1.call-done = f32[144,288]{1,0:T(8,128)} async-done(((f32[1152,288]{1,0:T(8,128)}), f32[144,288]{1,0:T(8,128)}) %reduce-scatter.23.cloned.1.call-update) | async-done | bytes 165904 | tf_op jit(solution)/shard_map/reduce_scatter | solution.py:242
  615.7 43.4 %reduce-scatter.25.cloned.1.call-done = f32[144,288]{1,0:T(8,128)} async-done(((f32[1152,288]{1,0:T(8,128)}), f32[144,288]{1,0:T(8,128)}) %reduce-scatter.25.cloned.1.call-update) | async-done | bytes 165904 | tf_op jit(solution)/shard_map/reduce_scatter | solution.py:243
  659.1 60.9 %reduce-scatter.33.cloned.1.call-done = f32[1076,144]{0,1:T(8,128)} async-done(((f32[1076,1152]{0,1:T(8,128)}), f32[1076,144]{0,1:T(8,128)}) %reduce-scatter.33.cloned.1.call-update) | async-done | bytes 619792 | tf_op jit(solution)/shard_map/reduce_scatter | solution.py:247
  720.1 61.2 %reduce-scatter.31.cloned.1.call-done = f32[144,1076]{1,0:T(8,128)} async-done(((f32[1152,1076]{1,0:T(8,128)}), f32[144,1076]{1,0:T(8,128)}) %reduce-scatter.31.cloned.1.call-update) | async-done | bytes 619792 | tf_op jit(solution)/shard_map/reduce_scatter | solution.py:246
  (164 shorter events, 27.4 us)
Async XLA Ops:
  8.0 52.6 %copy-start.27 = (s32[1,736]{1,0:T(1,128)S(1)}, s32[1,736]{1,0:T(1,128)}, u32[]{:S(2)}) copy-start(s32[1,736]{1,0:T(1,128)} %param.21) | copy-start | bytes 8836
  8.0 52.6 %copy-start.22 = (bf16[144,288]{1,0:T(8,128)(2,1)S(1)}, bf16[144,288]{1,0:T(8,128)(2,1)}, u32[]{:S(2)}) copy-start(bf16[144,288]{1,0:T(8,128)(2,1)} %param.22) | copy-start | bytes 248836
  8.0 63.7 %copy-start.23 = (bf16[144,288]{1,0:T(8,128)(2,1)S(1)}, bf16[144,288]{1,0:T(8,128)(2,1)}, u32[]{:S(2)}) copy-start(bf16[144,288]{1,0:T(8,128)(2,1)} %param.23) | copy-start | bytes 248836
  8.1 74.4 %copy-start.24 = (bf16[144,288]{1,0:T(8,128)(2,1)S(1)}, bf16[144,288]{1,0:T(8,128)(2,1)}, u32[]{:S(2)}) copy-start(bf16[144,288]{1,0:T(8,128)(2,1)} %param.24) | copy-start | bytes 248836
  8.1 84.3 %copy-start.25 = (bf16[288,144]{0,1:T(8,128)(2,1)S(1)}, bf16[288,144]{0,1:T(8,128)(2,1)}, u32[]{:S(2)}) copy-start(bf16[288,144]{0,1:T(8,128)(2,1)} %param.25) | copy-start | bytes 248836
  8.1 168.2 %reduce-scatter.35.cloned.1.call-start = ((), (), s32[]{:S(2)}) async-start(), calls=%async_computation.18 | async-start | bytes 2119680
  48.2 12.0 %collective-permute-start = (bf16[1,184,1152]{2,1,0:T(8,128)(2,1)S(1)}, bf16[1,184,1152]{2,1,0:T(8,128)(2,1)S(1)}, u32[]{:S(2)}, u32[]{:S(2)}) collective-permute-start(bf16[1,184,1152]{2,1,0:T(8,128)(2,1)S(1)} %fusion.50), channel_id=1, source_target_pairs={{0,3},{1,0},{2,1},{3,2},{4,7},{5,4},{6,5},{7,6},{8,11},{9,8},{10,9... | collective-permute-start | bytes 1271816 | tf_op jit(solution)/shard_map/ppermute | solution.py:19
  60.3 43.1 %collective-permute-start.1 = (bf16[1,368,1152]{2,1,0:T(8,128)(2,1)S(1)}, bf16[1,368,1152]{2,1,0:T(8,128)(2,1)}, u32[]{:S(2)}, u32[]{:S(2)}) collective-permute-start(bf16[1,368,1152]{2,1,0:T(8,128)(2,1)S(1)} %pad_maximum_fusion), channel_id=1, source_target_pairs={{0,2},{1,3},{2,0},{3,1},{4,6},{5,7},{6,4},{7,5},{8,10},{9,11},{10,... | collective-permute-start | bytes 2543624 | tf_op jit(solution)/shard_map/ppermute | solution.py:19
  71.7 39.0 %copy-start.4 = (bf16[1152,288]{1,0:T(8,128)(2,1)}, bf16[1152,288]{1,0:T(8,128)(2,1)S(1)}, u32[]{:S(2)}) copy-start(bf16[1152,288]{1,0:T(8,128)(2,1)S(1)} %all_gather.55) | copy-start | bytes 1990660
  82.4 28.3 %copy-start.6 = (bf16[1152,288]{1,0:T(8,128)(2,1)}, bf16[1152,288]{1,0:T(8,128)(2,1)S(1)}, u32[]{:S(2)}) copy-start(bf16[1152,288]{1,0:T(8,128)(2,1)S(1)} %all_gather.57) | copy-start | bytes 1990660
  103.4 26.4 %copy-start.18 = (bf16[288,1152]{0,1:T(8,128)(2,1)}, bf16[288,1152]{0,1:T(8,128)(2,1)S(1)}, u32[]{:S(2)}) copy-start(bf16[288,1152]{0,1:T(8,128)(2,1)S(1)} %all_gather.58) | copy-start | bytes 1990660
  109.9 5.2 copy-start.12
  110.8 2.6 copy-start.8
  113.3 3.5 copy-start.1
  116.0 1.0 copy-start.29
  129.8 0.8 copy-start.20
  129.8 4.4 copy-start.3
  129.8 46.4 %copy-start = (bf16[1,184,1152]{2,1,0:T(8,128)(2,1)S(1)}, bf16[1,184,1152]{2,1,0:T(8,128)(2,1)}, u32[]{:S(2)}) copy-start(bf16[1,184,1152]{2,1,0:T(8,128)(2,1)} %param.20) | copy-start | bytes 1271812
  133.0 140.3 %all-gather.3.cloned.1.call-start = ((), (), s32[]{:S(2)}) async-start(), calls=%async_computation.10 | async-start | bytes 2985984 | tf_op jit(solution)/shard_map/all_gather | solution.py:133
  133.5 146.6 %all-gather.5.cloned.1.call-start = ((), (), s32[]{:S(2)}) async-start(), calls=%async_computation.11 | async-start | bytes 2985984 | tf_op jit(solution)/shard_map/all_gather | solution.py:134
  134.1 197.4 %reduce-scatter.39.cloned.1.call-start = ((), (), s32[]{:S(2)}) async-start(), calls=%async_computation.20 | async-start | bytes 2119680
  134.2 49.3 %collective-permute-start.4 = (bf16[1,184,1152]{2,1,0:T(8,128)(2,1)S(1)}, bf16[1,184,1152]{2,1,0:T(8,128)(2,1)S(1)}, u32[]{:S(2)}, u32[]{:S(2)}) collective-permute-start(bf16[1,184,1152]{2,1,0:T(8,128)(2,1)S(1)} %copy-done.3), channel_id=1, source_target_pairs={{0,3},{1,0},{2,1},{3,2},{4,7},{5,4},{6,5},{7,6},{8,11},{9,8},{10,9... | collective-permute-start | bytes 1271816 | tf_op jit(solution)/shard_map/ppermute | solution.py:19
  180.1 13.6 %collective-permute-start.2 = (bf16[1,184,1152]{2,1,0:T(8,128)(2,1)S(1)}, bf16[1,184,1152]{2,1,0:T(8,128)(2,1)S(1)}, u32[]{:S(2)}, u32[]{:S(2)}) collective-permute-start(bf16[1,184,1152]{2,1,0:T(8,128)(2,1)S(1)} %add_convert_fusion.1), channel_id=1, source_target_pairs={{0,3},{1,0},{2,1},{3,2},{4,7},{5,4},{6,5},{7,6},{8,11},{9,8},{10,9... | collective-permute-start | bytes 1271816 | tf_op jit(solution)/shard_map/ppermute | solution.py:19
  184.5 64.1 %collective-permute-start.5 = (bf16[1,368,1152]{2,1,0:T(8,128)(2,1)}, bf16[1,368,1152]{2,1,0:T(8,128)(2,1)}, u32[]{:S(2)}, u32[]{:S(2)}) collective-permute-start(bf16[1,368,1152]{2,1,0:T(8,128)(2,1)} %pad_maximum_fusion.2), channel_id=1, source_target_pairs={{0,2},{1,3},{2,0},{3,1},{4,6},{5,7},{6,4},{7,5},{8,10},{9,11},{10,... | collective-permute-start | bytes 2543624 | tf_op jit(solution)/shard_map/ppermute | solution.py:19
  193.7 0.8 copy-start.16
  195.4 70.5 %collective-permute-start.3 = (bf16[1,368,1152]{2,1,0:T(8,128)(2,1)}, bf16[1,368,1152]{2,1,0:T(8,128)(2,1)}, u32[]{:S(2)}, u32[]{:S(2)}) collective-permute-start(bf16[1,368,1152]{2,1,0:T(8,128)(2,1)} %pad_maximum_fusion.1), channel_id=1, source_target_pairs={{0,2},{1,3},{2,0},{3,1},{4,6},{5,7},{6,4},{7,5},{8,10},{9,11},{10,... | collective-permute-start | bytes 2543624 | tf_op jit(solution)/shard_map/ppermute | solution.py:19
  196.3 69.6 %copy-start.17 = (bf16[1,184,1152]{2,1,0:T(8,128)(2,1)S(1)}, bf16[1,184,1152]{2,1,0:T(8,128)(2,1)}, u32[]{:S(2)}) copy-start(bf16[1,184,1152]{2,1,0:T(8,128)(2,1)} %copy-done.16) | copy-start | bytes 1271812
  280.1 9.4 %copy-start.28 = (bf16[1152,1076]{1,0:T(8,128)(2,1)S(1)}, bf16[1152,1076]{1,0:T(8,128)(2,1)}, u32[]{:S(2)}) copy-start(bf16[1152,1076]{1,0:T(8,128)(2,1)} %all-gather.3.cloned.1.call-done) | copy-start | bytes 7437316
  288.3 1.2 copy-start.31
  293.5 38.0 %copy-start.2 = (bf16[1,184,1152]{2,1,0:T(8,128)(2,1)S(1)}, bf16[1,184,1152]{2,1,0:T(8,128)(2,1)}, u32[]{:S(2)}) copy-start(bf16[1,184,1152]{2,1,0:T(8,128)(2,1)} %reduce-scatter.35.cloned.1.call-done) | copy-start | bytes 1271812
  293.5 77.1 %reduce-scatter.37.cloned.1.call-start = ((), (), s32[]{:S(2)}) async-start(), calls=%async_computation.19 | async-start | bytes 2119680
  300.8 185.4 %reduce-scatter.41.cloned.1.call-start = ((), (), s32[]{:S(2)}) async-start(), calls=%async_computation.21 | async-start | bytes 2119680
  370.6 66.2 %slice-start = ((s8[9043968]{0:T(1024)(128)(4,1)}), s8[4194304]{0:T(1024)(128)(4,1)S(1)}, s32[]{:S(2)}) async-start(s8[9043968]{0:T(1024)(128)(4,1)} %bitcast.89), calls=%async_computation.22 | async-start | bytes 8388608
  373.3 56.8 %copy-start.19 = (bf16[288,1152]{0,1:T(8,128)(2,1)S(1)}, bf16[288,1152]{0,1:T(8,128)(2,1)}, u32[]{:S(2)}) copy-start(bf16[288,1152]{0,1:T(8,128)(2,1)} %copy-done.18) | copy-start | bytes 1990660
  373.3 11.4 %collective-permute-start.6 = (bf16[1,184,1152]{2,1,0:T(8,128)(2,1)S(1)}, bf16[1,184,1152]{2,1,0:T(8,128)(2,1)S(1)}, u32[]{:S(2)}, u32[]{:S(2)}) collective-permute-start(bf16[1,184,1152]{2,1,0:T(8,128)(2,1)S(1)} %convert_element_type.180), channel_id=1, source_target_pairs={{0,3},{1,0},{2,1},{3,2},{4,7},{5,4},{6,5},{7,6},{8,11},{9,8},{10,9... | collective-permute-start | bytes 1271816 | tf_op jit(solution)/shard_map/ppermute | solution.py:19
  384.8 46.1 %copy-start.21 = (bf16[4,72,736]{2,1,0:T(8,128)(2,1)S(1)}, bf16[4,72,736]{2,1,0:T(8,128)(2,1)}, u32[]{:S(2)}) copy-start(bf16[4,72,736]{2,1,0:T(8,128)(2,1)} %copy-done.20) | copy-start | bytes 1271812
  384.8 52.0 %slice-start.1 = ((s8[9043968]{0:T(1024)(128)(4,1)}), s8[4194304]{0:T(1024)(128)(4,1)S(1)}, s32[]{:S(2)}) async-start(s8[9043968]{0:T(1024)(128)(4,1)} %bitcast.89), calls=%async_computation.23 | async-start | bytes 8388608
  384.8 38.7 %collective-permute-start.7 = (bf16[1,368,1152]{2,1,0:T(8,128)(2,1)S(1)}, bf16[1,368,1152]{2,1,0:T(8,128)(2,1)S(1)}, u32[]{:S(2)}, u32[]{:S(2)}) collective-permute-start(bf16[1,368,1152]{2,1,0:T(8,128)(2,1)S(1)} %pad_maximum_fusion.3), channel_id=1, source_target_pairs={{0,2},{1,3},{2,0},{3,1},{4,6},{5,7},{6,4},{7,5},{8,10},{9,11},{10,... | collective-permute-start | bytes 2543624 | tf_op jit(solution)/shard_map/ppermute | solution.py:19
  430.1 6.7 copy-start.15
  431.1 5.7 slice-start.2
  431.1 5.7 copy-start.30
  440.3 1.5 copy-start.9
  441.8 2.5 copy-start.10
  441.8 1.3 copy-start.5
  442.8 1.5 copy-start.7
  447.9 89.5 %reduce-scatter.29.cloned.1.call-start = ((), (), s32[]{:S(2)}) async-start(), calls=%async_computation.15 | async-start | bytes 1990656 | tf_op jit(solution)/shard_map/reduce_scatter | solution.py:245
  451.8 120.5 %reduce-scatter.27.cloned.1.call-start = ((), (), s32[]{:S(2)}) async-start(), calls=%async_computation.14 | async-start | bytes 1990656 | tf_op jit(solution)/shard_map/reduce_scatter | solution.py:244
  455.7 4.0 copy-start.11
  455.7 160.1 %reduce-scatter.23.cloned.1.call-start = ((), (), s32[]{:S(2)}) async-start(), calls=%async_computation.12 | async-start | bytes 1990656 | tf_op jit(solution)/shard_map/reduce_scatter | solution.py:242
  459.6 4.1 copy-start.14
  459.6 199.5 %reduce-scatter.25.cloned.1.call-start = ((), (), s32[]{:S(2)}) async-start(), calls=%async_computation.13 | async-start | bytes 1990656 | tf_op jit(solution)/shard_map/reduce_scatter | solution.py:243
  463.7 256.4 %reduce-scatter.33.cloned.1.call-start = ((), (), s32[]{:S(2)}) async-start(), calls=%async_computation.17 | async-start | bytes 5971968 | tf_op jit(solution)/shard_map/reduce_scatter | solution.py:247
  470.8 1.5 copy-start.13
  470.8 310.5 %reduce-scatter.31.cloned.1.call-start = ((), (), s32[]{:S(2)}) async-start(), calls=%async_computation.16 | async-start | bytes 5971968 | tf_op jit(solution)/shard_map/reduce_scatter | solution.py:246
  478.6 0.7 copy-start.26
Sparse Core Ops, SparseCore 0:
  133.1 43.1 reduce-scatter.34
  293.6 37.8 reduce-scatter.38
  333.9 36.6 reduce-scatter.36
  448.0 38.0 reduce-scatter.40
  490.0 39.3 reduce-scatter.28
  533.1 39.1 reduce-scatter.26
  576.3 39.4 reduce-scatter.22
  619.7 39.4 reduce-scatter.24
  663.1 56.9 reduce-scatter.32
  724.3 56.9 reduce-scatter.30
Sparse Core Ops, SparseCore 1:
  135.3 30.0 all-gather.2
  167.2 30.1 all-gather.4
